TPU v7x, 128 devices: a whole 4x4x4 slice. The times are simulated.
128 devices in a mesh: region: 16 (over y_lo, z, core), group: 8 (over y_hi, x).
Axes of the slice: x: 4, y: 4 (y_hi: 2, y_lo: 2; y = y_hi * 2 + y_lo), z: 4, core: 2. Of those that a mesh axis runs over, the one named last changes fastest.
Arguments:
- object_slab: float32 [8192, 2, 4096], P('region', None, 'group'), may hold values from -6 to 6
- probe: float32 [4, 2, 256, 256], replicated, may hold values from -6 to 6
- diffraction: float32 [512, 256, 256], P(('region', 'group')), may hold values from 0.25 to 16
- positions: int32 [512, 2], P(('region', 'group')), may hold values from 0 to 7936, as said below
- slot_counts: int32 [8, 16], P('group', 'region'), may hold values from 1 to 4, 40 in all within a row
Outputs:
- new_object: float32 [8192, 2, 4096], P('region', None, 'group')
- new_probe: float32 [4, 2, 256, 256], replicated
Inputs may be any that keep to these rules, and one draw needn't show every extreme that they name: `positions`: A slot of region index r has its row in r * 512 to min(r * 512 + 511, 7936); columns lie in 0 to 256; rows 0 and 7936 and columns 0 and 256 are each taken by some slot.
All inputs are finite; a program needn't handle non-finite values. No bound on the sum of `slot_counts` on one device may be relied on, other than what follows from the above.
Results may differ from a plain program's by a relative error of at most 0.0003.
Values sent between devices are 32-bit elements; how exact they have to be, the bound alone decides.
A program may use at most 128 MiB of HBM per device.

v0:
```python
import math
import jax
import jax.numpy as jnp
from jax import lax
from jax.sharding import PartitionSpec as P

highest = lax.Precision.HIGHEST


def shifted(block, axis, distance):
    devices = range(lax.axis_size(axis))
    route = [(i - distance, i) for i in devices if i - distance in devices]
    return lax.ppermute(block, axis, route)


def tables(side):
    index = jnp.arange(side, dtype=jnp.int32)
    prod = index[:, None] * index[None, :] % side
    angle = prod.astype(jnp.float32) * (2.0 * math.pi / side)
    scale = 1.0 / math.sqrt(side)
    return (jnp.cos(angle) * scale, -jnp.sin(angle) * scale)


def transform(real_part, imag_part, cos_tab, sin_tab):
    left_r = jnp.einsum("jk,mkl->mjl", cos_tab, real_part, precision=highest) - jnp.einsum(
        "jk,mkl->mjl", sin_tab, imag_part, precision=highest
    )
    left_i = jnp.einsum("jk,mkl->mjl", cos_tab, imag_part, precision=highest) + jnp.einsum(
        "jk,mkl->mjl", sin_tab, real_part, precision=highest
    )
    out_r = jnp.einsum("mjk,kl->mjl", left_r, cos_tab, precision=highest) - jnp.einsum(
        "mjk,kl->mjl", left_i, sin_tab, precision=highest
    )
    out_i = jnp.einsum("mjk,kl->mjl", left_r, sin_tab, precision=highest) + jnp.einsum(
        "mjk,kl->mjl", left_i, cos_tab, precision=highest
    )
    return (out_r, out_i)


def on_device(object_slab, probe, diffraction, positions, slot_counts):
    side = probe.shape[2]
    slots = diffraction.shape[0]
    tile_rows = object_slab.shape[0]
    active_count = slot_counts[0, 0]
    cos_tab, sin_tab = tables(side)
    base = lax.axis_index("region") * tile_rows
    local_rows = positions[:, 0] - base
    shard_columns = positions[:, 1]
    obj = object_slab
    prb = probe
    peak = jnp.max(jnp.sum(prb[:, 0] * prb[:, 0] + prb[:, 1] * prb[:, 1], axis=0))
    below = shifted(obj, "region", -1)
    extended = jnp.concatenate([obj, below], axis=0)

    def cut(row, col):
        return lax.dynamic_slice(extended, (row, jnp.int32(0), col), (side, 2, side))

    windows = jax.vmap(cut)(local_rows, shard_columns)
    probe_r = prb[:, 0]
    probe_i = prb[:, 1]

    def single_position(position_entry, carry):
        wgrads, pgrad, cover = carry
        live = (position_entry < active_count).astype(jnp.float32)
        win = lax.dynamic_index_in_dim(windows, position_entry, 0, keepdims=False)
        observed_intensity = lax.dynamic_index_in_dim(
            diffraction, position_entry, 0, keepdims=False
        )
        win_r = win[:, 0, :]
        win_i = win[:, 1, :]
        exit_r = probe_r * win_r[None] - probe_i * win_i[None]
        exit_i = probe_r * win_i[None] + probe_i * win_r[None]
        far_r, far_i = transform(exit_r, exit_i, cos_tab, sin_tab)
        model_intensity = jnp.sum(far_r * far_r + far_i * far_i, axis=0)
        update_ratio = 1.0 - jnp.sqrt(observed_intensity) / jnp.sqrt(
            jnp.maximum(model_intensity, 1.0)
        )
        chi_r, chi_i = transform(
            far_r * update_ratio[None], far_i * update_ratio[None], cos_tab, -sin_tab
        )
        chi_r = chi_r * live
        chi_i = chi_i * live
        go_r = jnp.sum(probe_r * chi_r + probe_i * chi_i, axis=0)
        go_i = jnp.sum(probe_r * chi_i - probe_i * chi_r, axis=0)
        grad_win = jnp.stack([go_r, go_i], axis=1)
        wgrads = lax.dynamic_update_index_in_dim(wgrads, grad_win, position_entry, 0)
        gp = jnp.stack(
            [win_r[None] * chi_r + win_i[None] * chi_i, win_r[None] * chi_i - win_i[None] * chi_r],
            axis=1,
        )
        return (wgrads, pgrad + gp, cover + live * (win_r * win_r + win_i * win_i))

    start_carry = (
        jnp.zeros((slots, side, 2, side), jnp.float32),
        jnp.zeros(prb.shape, jnp.float32),
        jnp.zeros((side, side), jnp.float32),
    )
    wgrads, pgrad, cover = lax.fori_loop(0, slots, single_position, start_carry)
    pgrad, cover = lax.psum((pgrad, cover), ("region", "group"))

    def put(position_entry, scratch_array):
        row = local_rows[position_entry]
        col = shard_columns[position_entry]
        current = lax.dynamic_slice(scratch_array, (row, jnp.int32(0), col), (side, 2, side))
        return lax.dynamic_update_slice(
            scratch_array, current + wgrads[position_entry], (row, jnp.int32(0), col)
        )

    scratch_array = lax.fori_loop(0, slots, put, jnp.zeros(extended.shape, jnp.float32))
    tile_grad = scratch_array[:tile_rows]
    spill = scratch_array[tile_rows:]
    arrived = shifted(spill, "region", 1)
    tile_grad = tile_grad + arrived
    obj = obj - tile_grad / peak
    prb = prb - pgrad / (cover + 1e-06)[None, None]
    return (obj, prb)


def solution(mesh):
    placed = (
        P("region", None, "group"),
        P(),
        P(("region", "group"), None, None),
        P(("region", "group"), None),
        P("group", "region"),
    )
    return jax.shard_map(
        on_device,
        mesh=mesh,
        in_specs=placed,
        out_specs=(P("region", None, "group"), P()),
        check_vma=False,
    )
```

profile of v0, /device:TPU:1, one launch (start us, length us, event | category | flops | bytes accessed | tf_op | source)
XLA Modules:
  0.0 704.6 jit_solution(1375702932699397892)
XLA Ops:
  7.2 3.3 collective-permute-start
  13.6 22.5 %collective-permute-done = f32[512,2,512]{2,1,0:T(2,128)} collective-permute-done((f32[512,2,512]{2,1,0:T(2,128)}, f32[512,2,512]{2,1,0:T(2,128)}, u32[]{:S(2)}, u32[]{:S(2)}) %collective-permute-start) | collective-permute-done | bytes 2097184 | tf_op jit(solution)/shard_map/ppermute | solution.py:13
  36.2 5.3 pad_maximum_fusion
  43.4 17.1 %while.35 = (s32[]{:T(128)}, f32[1024,2,512]{2,1,0:T(2,128)}, s32[4,3]{1,0:T(4,128)S(1)}, f32[4,256,2,256]{3,2,1,0:T(2,128)}, s32[]{:T(128)}) while((s32[]{:T(128)}, f32[1024,2,512]{2,1,0:T(2,128)}, s32[4,3]{1,0:T(4,128)S(1)}, f32[4,256,2,256]{3,2,1,0:T(2,128)}, s32[]{:T(128)}) %tuple.99), condition=%wide.while_cond, body=%wide.while_body.sunk | while | flops 2 | bytes 1050217 | solution.py:56
  43.9 3.7 bitcast_dynamic-update-slice_fusion.2
  48.2 3.7 bitcast_dynamic-update-slice_fusion.2
  52.5 3.7 bitcast_dynamic-update-slice_fusion.2
  56.8 3.7 bitcast_dynamic-update-slice_fusion.2
  62.3 249.9 %while.36 = (s32[]{:T(128)}, f32[4,256,2,256]{3,2,1,0:T(2,128)}, f32[4,2,256,256]{3,2,0,1:T(8,128)}, f32[256,256]{1,0:T(8,128)}, f32[4,256,2,256]{3,2,1,0:T(2,12...) while((s32[]{:T(128)}, f32[4,256,2,256]{3,2,1,0:T(2,128)}, ...), condition=%wide.region_4.5_spmd.clone.clone, body=%wide.region_0.4_spmd.clone.clone.sunk | while | flops 12915048448 | bytes 82838280 | solution.py:98
  63.9 2.7 fusion.223
  66.7 2.7 fusion.224
  69.4 2.7 fusion.220
  72.1 2.7 fusion.221
  74.9 3.2 fusion.222
  87.2 2.8 fusion.230
  90.0 3.7 fusion.231
  100.1 3.7 fusion.229
  104.4 4.6 fusion.232
  111.7 5.4 add_bitcast_fusion.2
  117.0 3.2 maximum_add_fusion.2
  124.3 2.7 fusion.223
  127.1 2.7 fusion.224
  129.8 2.7 fusion.220
  132.5 2.7 fusion.221
  135.3 2.8 fusion.222
  143.5 2.7 add_reduce_fusion.4
  147.2 2.9 fusion.230
  150.1 3.7 fusion.231
  160.1 3.7 fusion.229
  164.5 4.8 fusion.232
  172.0 5.4 add_bitcast_fusion.2
  177.3 3.9 maximum_add_fusion.2
  186.0 2.7 fusion.223
  188.7 2.7 fusion.224
  191.5 2.7 fusion.220
  194.2 2.7 fusion.221
  197.0 2.9 fusion.222
  208.9 3.1 fusion.230
  212.0 3.7 fusion.231
  222.1 3.7 fusion.229
  226.4 4.5 fusion.232
  233.6 5.4 add_bitcast_fusion.2
  239.0 3.9 maximum_add_fusion.2
  247.7 2.7 fusion.223
  250.5 2.7 fusion.224
  253.2 2.7 fusion.220
  255.9 2.7 fusion.221
  258.7 3.1 fusion.222
  270.8 2.8 fusion.230
  273.7 3.7 fusion.231
  283.7 3.7 fusion.229
  288.1 4.6 fusion.232
  295.3 5.4 add_bitcast_fusion.2
  300.7 3.9 maximum_add_fusion.2
  312.3 3.0 broadcast_in_dim.30
  315.3 207.1 %while.34 = (s32[]{:T(128)}, f32[1024,2,512]{2,1,0:T(2,128)}, s32[4]{0:T(128)S(1)}, s32[4]{0:T(128)S(1)}, f32[4,256,2,256]{3,2,1,0:T(2,128)}, /*index=5*/s32[]{:T(128)}, s32[]{:T(128)}, s32[]{:T(128)}, s32[]{:T(128)}) while((s32[]{:T(128)}, f32[1024,2,512]{2,1,0:T(2,128)}, s32[4]{0:T(128)S(1)}, s32[4]{0:T(128)S(1)}, ...), condition=%wide.region_6.7_spmd, body=%wide.region_5.6_spmd.sunk | while | flops 131080 | bytes 2621641 | solution.py:109
  322.1 45.0 %dynamic_update_slice.21 = f32[1024,2,512]{2,1,0:T(2,128)} dynamic-update-slice(f32[1024,2,512]{2,1,0:T(2,128)} %get-tuple-element.735, f32[256,2,256]{2,1,0:T(2,128)S(1)} %bitcast_add_fusion.2, s32[]{:T(128)S(6)} %select_n.175, s32[]{:T(128)} %constant.116.clone.1..sunk, s32[]{:T(128)S(6)} %select_n.176) | dynamic-update-slice | bytes 1048580 | tf_op jit(solution)/shard_map/while/body/eval_jaxpr/dynamic_update_slice | solution.py:105
  373.8 45.0 %dynamic_update_slice.21 = f32[1024,2,512]{2,1,0:T(2,128)} dynamic-update-slice(f32[1024,2,512]{2,1,0:T(2,128)} %get-tuple-element.735, f32[256,2,256]{2,1,0:T(2,128)S(1)} %bitcast_add_fusion.2, s32[]{:T(128)S(6)} %select_n.175, s32[]{:T(128)} %constant.116.clone.1..sunk, s32[]{:T(128)S(6)} %select_n.176) | dynamic-update-slice | bytes 1048580 | tf_op jit(solution)/shard_map/while/body/eval_jaxpr/dynamic_update_slice | solution.py:105
  425.6 45.0 %dynamic_update_slice.21 = f32[1024,2,512]{2,1,0:T(2,128)} dynamic-update-slice(f32[1024,2,512]{2,1,0:T(2,128)} %get-tuple-element.735, f32[256,2,256]{2,1,0:T(2,128)S(1)} %bitcast_add_fusion.2, s32[]{:T(128)S(6)} %select_n.175, s32[]{:T(128)} %constant.116.clone.1..sunk, s32[]{:T(128)S(6)} %select_n.176) | dynamic-update-slice | bytes 1048580 | tf_op jit(solution)/shard_map/while/body/eval_jaxpr/dynamic_update_slice | solution.py:105
  477.4 45.0 %dynamic_update_slice.21 = f32[1024,2,512]{2,1,0:T(2,128)} dynamic-update-slice(f32[1024,2,512]{2,1,0:T(2,128)} %get-tuple-element.735, f32[256,2,256]{2,1,0:T(2,128)S(1)} %bitcast_add_fusion.2, s32[]{:T(128)S(6)} %select_n.175, s32[]{:T(128)} %constant.116.clone.1..sunk, s32[]{:T(128)S(6)} %select_n.176) | dynamic-update-slice | bytes 1048580 | tf_op jit(solution)/shard_map/while/body/eval_jaxpr/dynamic_update_slice | solution.py:105
  522.3 3.8 slice.43
  532.0 155.4 %all-reduce.3.cloned.1.call-done = (f32[4,2,256,256]{3,2,1,0:T(8,128)}, f32[256,256]{1,0:T(8,128)}) async-done(((f32[4,2,256,256]{3,2,1,0:T(8,128)}, f32[256,256]{1,0:T(8,128)}), (f32[4,2,256,256]{3,2,1,0:T(8,128)}, f32[256,256]{1,0:T(8,128)})) %all-reduce.3.cloned.1.call-update) | async-done | bytes 2359312 | tf_op jit(solution)/shard_map/psum | solution.py:99
  688.5 3.4 divide_subtract_fusion.1
  692.7 4.9 divide_subtract_fusion
  (137 shorter events, 116.7 us)
Async XLA Ops:
  7.2 680.3 %all-reduce.3.cloned.1.call-start = ((), (), s32[]{:S(2)}) async-start(), calls=%async_computation | async-start | bytes 4718592 | tf_op jit(solution)/shard_map/psum | solution.py:99
  7.2 29.0 %collective-permute-start = (f32[512,2,512]{2,1,0:T(2,128)}, f32[512,2,512]{2,1,0:T(2,128)}, u32[]{:S(2)}, u32[]{:S(2)}) collective-permute-start(f32[512,2,512]{2,1,0:T(2,128)} %param.9), channel_id=1, source_target_pairs={{8,0},{16,8},{24,16},{32,24},{40,32},{48,40},{56,48},{64,56},{72,6... | collective-permute-start | bytes 6291464 | tf_op jit(solution)/shard_map/ppermute | solution.py:13
  11.7 24.5 %copy-start.7 = (f32[512,2,512]{2,1,0:T(2,128)S(1)}, f32[512,2,512]{2,1,0:T(2,128)}, u32[]{:S(2)}) copy-start(f32[512,2,512]{2,1,0:T(2,128)} %param.9) | copy-start | bytes 6291460
  99.0 1.0 copy-start.1
  104.4 4.6 copy-start.2
  104.4 7.3 %copy-start = (f32[4,256,256]{1,2,0:T(8,128)S(1)}, f32[4,256,256]{1,2,0:T(8,128)}, u32[]{:S(2)}) copy-start(f32[4,256,256]{1,2,0:T(8,128)} %fusion.231) | copy-start | bytes 3145732 | tf_op jit(solution)/shard_map/while
  117.0 3.2 copy-start.5
  159.1 1.0 copy-start.1
  164.5 4.8 copy-start.2
  164.5 7.5 %copy-start = (f32[4,256,256]{1,2,0:T(8,128)S(1)}, f32[4,256,256]{1,2,0:T(8,128)}, u32[]{:S(2)}) copy-start(f32[4,256,256]{1,2,0:T(8,128)} %fusion.231) | copy-start | bytes 3145732 | tf_op jit(solution)/shard_map/while
  177.3 3.9 copy-start.5
  221.0 1.0 copy-start.1
  226.4 4.6 copy-start.2
  226.4 7.2 %copy-start = (f32[4,256,256]{1,2,0:T(8,128)S(1)}, f32[4,256,256]{1,2,0:T(8,128)}, u32[]{:S(2)}) copy-start(f32[4,256,256]{1,2,0:T(8,128)} %fusion.231) | copy-start | bytes 3145732 | tf_op jit(solution)/shard_map/while
  239.0 3.9 copy-start.5
  282.7 1.0 copy-start.1
  288.0 4.6 copy-start.2
  288.1 7.3 %copy-start = (f32[4,256,256]{1,2,0:T(8,128)S(1)}, f32[4,256,256]{1,2,0:T(8,128)}, u32[]{:S(2)}) copy-start(f32[4,256,256]{1,2,0:T(8,128)} %fusion.231) | copy-start | bytes 3145732 | tf_op jit(solution)/shard_map/while
  300.7 3.9 copy-start.5
  522.3 5.7 copy-start.3
  526.2 165.7 %collective-permute-start.1 = (f32[512,2,512]{2,1,0:T(2,128)}, f32[512,2,512]{2,1,0:T(2,128)}, u32[]{:S(2)}, u32[]{:S(2)}) collective-permute-start(f32[512,2,512]{2,1,0:T(2,128)} %slice.43), channel_id=1, source_target_pairs={{0,8},{8,16},{16,24},{24,32},{32,40},{40,48},{48,56},{56,64},{64,7... | collective-permute-start | bytes 6291464 | tf_op jit(solution)/shard_map/ppermute | solution.py:13
  529.6 1.6 copy-start.6
  688.4 3.4 copy-start.4
  688.4 4.2 copy-start.8
Sparse Core Ops, SparseCore 0:
  529.8 157.6 all-reduce.2
where the time goes:
time: 710 us; the launch traced here: 705 us
  local copies, waits for them, and re-layouts  230 us (32%)
  matrix products  201 us (28%)
  waiting for transfers between devices  178 us (25%)
  other arithmetic  53.2 us (7%)
  loops' own time  23.3 us (3%)
  between operations  14.3 us (2%)
    dynamic_update_slice x4, local copies, waits for them, and re-layouts, put(): lax.dynamic_update_slice(scratch_array, current + wgrads[position_entry],...  180 us
    psum x1, waiting for transfers between devices, on_device(): pgrad, cover = lax.psum((pgrad, cover), ('region', 'group'))  155 us
    dot_general x8, matrix products, transform(): jnp.einsum('mjk,kl->mjl', left_i, sin_tab, precision=highest)  32.1 us
    dot_general x8, matrix products, transform(): jnp.einsum('mjk,kl->mjl', left_i, cos_tab, precision=highest)  29.2 us
    dot_general x8, matrix products, transform(): jnp.einsum('jk,mkl->mjl', sin_tab, real_part, precision=highest)  25.5 us
    dot_general x8, matrix products, transform(): jnp.einsum('mjk,kl->mjl', left_r, sin_tab, precision=highest)  25.3 us
    dot_general x8, matrix products, transform(): jnp.einsum('mjk,kl->mjl', left_r, cos_tab, precision=highest)  22.6 us
    ppermute x2, waiting for transfers between devices, shifted(): return lax.ppermute(block, axis, route)  22.5 us
  transfers between devices with their start and end apart: 3, of which 2 were waited for; matrix products, arithmetic and copies ran while one was open for 1% of the time, Pallas kernels for 0%

commit v1 on v0

--- a/solution.py
+++ b/solution.py
@@ -3,8 +3,15 @@
 import jax.numpy as jnp
 from jax import lax
 from jax.sharding import PartitionSpec as P
+from jax.lax import psum
 
 highest = lax.Precision.HIGHEST
+
+
+def open_ports_in(patch):
+    y_new = psum(patch, axis_name="group")
+    ready = psum(y_new, axis_name="region")
+    return ready
 
 
 def shifted(block, axis, distance):
@@ -96,7 +103,7 @@
         jnp.zeros((side, side), jnp.float32),
     )
     wgrads, pgrad, cover = lax.fori_loop(0, slots, single_position, start_carry)
-    pgrad, cover = lax.psum((pgrad, cover), ("region", "group"))
+    pgrad, cover = open_ports_in((pgrad, cover))
 
     def put(position_entry, scratch_array):
         row = local_rows[position_entry]

time: 710 us -> 680 us (0.958)
  waiting for transfers between devices: 178 us -> 145 us
    psum x1 -> x2, waiting for transfers between devices: 155 us -> 97.2 us  [the longest x1 97.1 us: open_ports_in(): ready = psum(y_new, axis_name='region')]
    ppermute x2, waiting for transfers between devices: 22.5 us -> 48.1 us  [shifted(): return lax.ppermute(block, axis, route)]
  transfers between devices with their start and end apart: 3 -> 4, of which waited for: 2 -> 3; matrix products, arithmetic and copies ran while one was open for 1% -> 31% of each run, Pallas kernels for 0% -> 0%
where the time goes in v1:
time: 680 us; the launch traced here: 674 us
  local copies, waits for them, and re-layouts  230 us (34%)
  matrix products  200 us (29%)
  waiting for transfers between devices  145 us (21%)
  other arithmetic  53.4 us (8%)
  loops' own time  25 us (4%)
  between operations  14.3 us (2%)
    dynamic_update_slice x4, local copies, waits for them, and re-layouts, put(): lax.dynamic_update_slice(scratch_array, current + wgrads[position_entry],...  180 us
    psum x1, waiting for transfers between devices, open_ports_in(): ready = psum(y_new, axis_name='region')  97.1 us
    ppermute x2, waiting for transfers between devices, shifted(): return lax.ppermute(block, axis, route)  48.1 us
    dot_general x8, matrix products, transform(): jnp.einsum('mjk,kl->mjl', left_i, sin_tab, precision=highest)  32.1 us
    dot_general x8, matrix products, transform(): jnp.einsum('mjk,kl->mjl', left_i, cos_tab, precision=highest)  29.2 us
    dot_general x8, matrix products, transform(): jnp.einsum('jk,mkl->mjl', sin_tab, real_part, precision=highest)  25.5 us
    dot_general x8, matrix products, transform(): jnp.einsum('mjk,kl->mjl', left_r, sin_tab, precision=highest)  25.3 us
    dot_general x8, matrix products, transform(): jnp.einsum('mjk,kl->mjl', left_r, cos_tab, precision=highest)  22.6 us
  transfers between devices with their start and end apart: 4, of which 3 were waited for; matrix products, arithmetic and copies ran while one was open for 31% of the time, Pallas kernels for 0%

profile of v1, /device:TPU:1, one launch (start us, length us, event | category | flops | bytes accessed | tf_op | source)
XLA Modules:
  0.0 673.8 jit_solution(14196540047757797009)
XLA Ops:
  7.2 3.3 collective-permute-start
  13.6 22.5 %collective-permute-done = f32[512,2,512]{2,1,0:T(2,128)} collective-permute-done((f32[512,2,512]{2,1,0:T(2,128)}, f32[512,2,512]{2,1,0:T(2,128)}, u32[]{:S(2)}, u32[]{:S(2)}) %collective-permute-start) | collective-permute-done | bytes 2097184 | tf_op jit(solution)/shard_map/ppermute | solution.py:20
  36.2 5.3 pad_maximum_fusion
  43.4 17.9 %while.35 = (s32[]{:T(128)}, f32[1024,2,512]{2,1,0:T(2,128)}, s32[4,3]{1,0:T(4,128)S(1)}, f32[4,256,2,256]{3,2,1,0:T(2,128)}, s32[]{:T(128)}) while((s32[]{:T(128)}, f32[1024,2,512]{2,1,0:T(2,128)}, s32[4,3]{1,0:T(4,128)S(1)}, f32[4,256,2,256]{3,2,1,0:T(2,128)}, s32[]{:T(128)}) %tuple.99), condition=%wide.while_cond, body=%wide.while_body.sunk | while | flops 2 | bytes 1050217 | solution.py:63
  44.0 3.8 bitcast_dynamic-update-slice_fusion.2
  48.5 3.8 bitcast_dynamic-update-slice_fusion.2
  53.0 3.8 bitcast_dynamic-update-slice_fusion.2
  57.4 3.8 bitcast_dynamic-update-slice_fusion.2
  63.1 249.8 %while.36 = (s32[]{:T(128)}, f32[4,256,2,256]{3,2,1,0:T(2,128)}, f32[4,2,256,256]{3,2,0,1:T(8,128)}, f32[256,256]{1,0:T(8,128)}, f32[4,256,2,256]{3,2,1,0:T(2,12...) while((s32[]{:T(128)}, f32[4,256,2,256]{3,2,1,0:T(2,128)}, ...), condition=%wide.region_4.5_spmd.clone.clone, body=%wide.region_0.4_spmd.clone.clone.sunk | while | flops 12915048448 | bytes 82838280 | solution.py:105
  67.4 2.7 fusion.224
  70.2 2.7 fusion.220
  72.9 2.7 fusion.221
  75.6 3.2 fusion.222
  87.9 2.8 fusion.230
  90.8 3.6 fusion.231
  100.8 3.7 fusion.229
  105.1 4.6 fusion.232
  112.4 5.3 add_bitcast_fusion.2
  117.8 3.2 maximum_add_fusion.2
  125.0 2.7 fusion.223
  127.8 2.7 fusion.224
  130.5 2.7 fusion.220
  133.3 2.7 fusion.221
  136.0 2.8 fusion.222
  147.9 2.9 fusion.230
  150.8 3.6 fusion.231
  160.8 3.7 fusion.229
  165.2 4.8 fusion.232
  172.7 5.3 add_bitcast_fusion.2
  178.0 3.9 maximum_add_fusion.2
  186.7 2.7 fusion.223
  189.4 2.7 fusion.224
  192.2 2.7 fusion.220
  194.9 2.7 fusion.221
  197.6 2.9 fusion.222
  209.6 3.1 fusion.230
  212.7 3.6 fusion.231
  222.7 3.7 fusion.229
  227.1 4.5 fusion.232
  234.3 5.3 add_bitcast_fusion.2
  239.6 3.9 maximum_add_fusion.2
  248.4 2.7 fusion.223
  251.1 2.7 fusion.224
  253.9 2.7 fusion.220
  256.6 2.7 fusion.221
  259.3 3.1 fusion.222
  271.5 2.8 fusion.230
  274.4 3.6 fusion.231
  284.4 3.7 fusion.229
  288.7 4.6 fusion.232
  296.0 5.3 add_bitcast_fusion.2
  301.3 3.9 maximum_add_fusion.2
  312.9 3.1 copy.72
  316.1 3.0 broadcast_in_dim.30
  319.1 209.1 %while.34 = (s32[]{:T(128)}, f32[1024,2,512]{2,1,0:T(2,128)}, s32[4]{0:T(128)S(1)}, s32[4]{0:T(128)S(1)}, f32[4,256,2,256]{3,2,1,0:T(2,128)}, /*index=5*/s32[]{:T(128)}, s32[]{:T(128)}, s32[]{:T(128)}, s32[]{:T(128)}) while((s32[]{:T(128)}, f32[1024,2,512]{2,1,0:T(2,128)}, s32[4]{0:T(128)S(1)}, s32[4]{0:T(128)S(1)}, ...), condition=%wide.region_6.7_spmd, body=%wide.region_5.6_spmd.sunk | while | flops 131080 | bytes 2621641 | solution.py:116
  326.4 45.0 %dynamic_update_slice.21 = f32[1024,2,512]{2,1,0:T(2,128)} dynamic-update-slice(f32[1024,2,512]{2,1,0:T(2,128)} %get-tuple-element.737, f32[256,2,256]{2,1,0:T(2,128)S(1)} %bitcast_add_fusion.2, s32[]{:T(128)S(6)} %select_n.175, s32[]{:T(128)} %constant.116.clone.1..sunk, s32[]{:T(128)S(6)} %select_n.176) | dynamic-update-slice | bytes 1048580 | tf_op jit(solution)/shard_map/while/body/eval_jaxpr/dynamic_update_slice | solution.py:112
  378.7 45.0 %dynamic_update_slice.21 = f32[1024,2,512]{2,1,0:T(2,128)} dynamic-update-slice(f32[1024,2,512]{2,1,0:T(2,128)} %get-tuple-element.737, f32[256,2,256]{2,1,0:T(2,128)S(1)} %bitcast_add_fusion.2, s32[]{:T(128)S(6)} %select_n.175, s32[]{:T(128)} %constant.116.clone.1..sunk, s32[]{:T(128)S(6)} %select_n.176) | dynamic-update-slice | bytes 1048580 | tf_op jit(solution)/shard_map/while/body/eval_jaxpr/dynamic_update_slice | solution.py:112
  430.9 45.0 %dynamic_update_slice.21 = f32[1024,2,512]{2,1,0:T(2,128)} dynamic-update-slice(f32[1024,2,512]{2,1,0:T(2,128)} %get-tuple-element.737, f32[256,2,256]{2,1,0:T(2,128)S(1)} %bitcast_add_fusion.2, s32[]{:T(128)S(6)} %select_n.175, s32[]{:T(128)} %constant.116.clone.1..sunk, s32[]{:T(128)S(6)} %select_n.176) | dynamic-update-slice | bytes 1048580 | tf_op jit(solution)/shard_map/while/body/eval_jaxpr/dynamic_update_slice | solution.py:112
  483.2 45.0 %dynamic_update_slice.21 = f32[1024,2,512]{2,1,0:T(2,128)} dynamic-update-slice(f32[1024,2,512]{2,1,0:T(2,128)} %get-tuple-element.737, f32[256,2,256]{2,1,0:T(2,128)S(1)} %bitcast_add_fusion.2, s32[]{:T(128)S(6)} %select_n.175, s32[]{:T(128)} %constant.116.clone.1..sunk, s32[]{:T(128)S(6)} %select_n.176) | dynamic-update-slice | bytes 1048580 | tf_op jit(solution)/shard_map/while/body/eval_jaxpr/dynamic_update_slice | solution.py:112
  528.1 3.6 slice.43
  534.7 25.6 %collective-permute-done.1 = f32[512,2,512]{2,1,0:T(2,128)} collective-permute-done((f32[512,2,512]{2,1,0:T(2,128)}, f32[512,2,512]{2,1,0:T(2,128)}, u32[]{:S(2)}, u32[]{:S(2)}) %collective-permute-start.1) | collective-permute-done | bytes 2097184 | tf_op jit(solution)/shard_map/ppermute | solution.py:20
  560.3 5.2 divide_subtract_fusion
  565.5 97.1 %all-reduce.5.cloned.1.call-done = (f32[4,2,256,256]{3,2,1,0:T(8,128)}, f32[256,256]{1,0:T(8,128)}) async-done(((f32[4,2,256,256]{3,2,1,0:T(8,128)}, f32[256,256]{1,0:T(8,128)}), (f32[4,2,256,256]{3,2,1,0:T(8,128)}, f32[256,256]{1,0:T(8,128)})) %all-reduce.5.cloned.1.call-update) | async-done | bytes 2359312 | tf_op jit(solution)/shard_map/psum | solution.py:13
  663.6 3.2 divide_subtract_fusion.1
  (134 shorter events, 119.0 us)
Async XLA Ops:
  7.2 526.7 %all-reduce.7.cloned.1.call-start = ((), (), s32[]{:S(2)}) async-start(), calls=%async_computation.1 | async-start | bytes 4718592 | tf_op jit(solution)/shard_map/psum | solution.py:12
  7.2 29.0 %collective-permute-start = (f32[512,2,512]{2,1,0:T(2,128)}, f32[512,2,512]{2,1,0:T(2,128)}, u32[]{:S(2)}, u32[]{:S(2)}) collective-permute-start(f32[512,2,512]{2,1,0:T(2,128)} %param.9), channel_id=1, source_target_pairs={{8,0},{16,8},{24,16},{32,24},{40,32},{48,40},{56,48},{64,56},{72,6... | collective-permute-start | bytes 6291464 | tf_op jit(solution)/shard_map/ppermute | solution.py:20
  11.7 24.5 %copy-start.5 = (f32[512,2,512]{2,1,0:T(2,128)S(1)}, f32[512,2,512]{2,1,0:T(2,128)}, u32[]{:S(2)}) copy-start(f32[512,2,512]{2,1,0:T(2,128)} %param.9) | copy-start | bytes 6291460
  99.8 1.0 copy-start.1
  105.1 4.6 copy-start.2
  105.1 7.3 %copy-start = (f32[4,256,256]{1,2,0:T(8,128)S(1)}, f32[4,256,256]{1,2,0:T(8,128)}, u32[]{:S(2)}) copy-start(f32[4,256,256]{1,2,0:T(8,128)} %fusion.231) | copy-start | bytes 3145732 | tf_op jit(solution)/shard_map/while
  117.8 3.2 copy-start.3
  159.8 1.0 copy-start.1
  165.2 4.8 copy-start.2
  165.2 7.5 %copy-start = (f32[4,256,256]{1,2,0:T(8,128)S(1)}, f32[4,256,256]{1,2,0:T(8,128)}, u32[]{:S(2)}) copy-start(f32[4,256,256]{1,2,0:T(8,128)} %fusion.231) | copy-start | bytes 3145732 | tf_op jit(solution)/shard_map/while
  178.0 3.9 copy-start.3
  221.7 1.0 copy-start.1
  227.0 4.6 copy-start.2
  227.1 7.2 %copy-start = (f32[4,256,256]{1,2,0:T(8,128)S(1)}, f32[4,256,256]{1,2,0:T(8,128)}, u32[]{:S(2)}) copy-start(f32[4,256,256]{1,2,0:T(8,128)} %fusion.231) | copy-start | bytes 3145732 | tf_op jit(solution)/shard_map/while
  239.6 3.9 copy-start.3
  283.4 1.0 copy-start.1
  288.7 4.6 copy-start.2
  288.7 7.3 %copy-start = (f32[4,256,256]{1,2,0:T(8,128)S(1)}, f32[4,256,256]{1,2,0:T(8,128)}, u32[]{:S(2)}) copy-start(f32[4,256,256]{1,2,0:T(8,128)} %fusion.231) | copy-start | bytes 3145732 | tf_op jit(solution)/shard_map/while
  301.3 3.9 copy-start.3
  316.0 346.6 %all-reduce.5.cloned.1.call-start = ((), (), s32[]{:S(2)}) async-start(), calls=%async_computation | async-start | bytes 4718592 | tf_op jit(solution)/shard_map/psum | solution.py:13
  531.8 2.1 copy-start.4
  531.8 28.5 %collective-permute-start.1 = (f32[512,2,512]{2,1,0:T(2,128)}, f32[512,2,512]{2,1,0:T(2,128)}, u32[]{:S(2)}, u32[]{:S(2)}) collective-permute-start(f32[512,2,512]{2,1,0:T(2,128)} %slice.43), channel_id=1, source_target_pairs={{0,8},{8,16},{16,24},{24,32},{32,40},{40,48},{48,56},{56,64},{64,7... | collective-permute-start | bytes 6291464 | tf_op jit(solution)/shard_map/ppermute | solution.py:20
Sparse Core Ops, SparseCore 0:
  316.1 94.2 all-reduce.6
  534.0 128.5 all-reduce.4
